TPU v7x, 512 devices: a whole 4x4x16 slice. The times are simulated.
512 devices in a mesh: section: 4 (over x), dp: 4 (over y), tensor: 32 (over z, core).
Axes of the slice: x: 4, y: 4, z: 16, core: 2. Of those that a mesh axis runs over, the one named last changes fastest.
Arguments:
- activations: bfloat16 [512, 8192], P('dp', 'tensor'), may hold values from -6 to 6
- targets: bfloat16 [4, 512, 8192], P('section', 'dp', 'tensor'), may hold values from -12 to 12
- packed_floors: int32 [4, 2048, 8192], P('section', 'dp', 'tensor'), may hold values from 0 to 4095
- rounding: float32 [4, 8192, 8192], P('section', 'dp', 'tensor'), may hold values from -8 to 8
- scales: float32 [4, 8192], P('section', 'tensor'), may hold values from 0.001 to 0.006
- norm_gains: float32 [4, 8192], P('section'), may hold values from 0.5 to 1.5
Outputs:
- rounding_next: float32 [4, 8192, 8192], P('section', 'dp', 'tensor')
- block_outputs: bfloat16 [4, 512, 8192], P('section', 'dp', 'tensor')
- losses: float32 [4], P('section')
Inputs may be any that keep to these rules, and one draw needn't show every extreme that they name: `packed_floors`: each word holds four 3-bit codes in its lowest 12 bits, lowest bits first: code k of word r of a column is row 4 r + k; the floor is the code minus 4.
All inputs are finite; a program needn't handle non-finite values.
Results may differ from a plain program's by a relative error of at most 0.0045.
The roundings to bfloat16 on the way count: a program that leaves them out, or rounds other values in their place, can miss the bound.
Values may be sent and summed in bfloat16 or wider, within the bound.
No kernel may reach another device: no remote copies, remote signals or barrier semaphores. Data moves between devices by JAX's collectives and lax.ppermute only.
A program may use at most 64 MiB of HBM per device.

v0:
```python
import jax
import jax.numpy as jnp
from jax import lax
from jax.sharding import Mesh
from jax.sharding import PartitionSpec as P

TENSOR = ("tensor_0", "tensor_1")
PLANE = ("section", "dp")
norm_eps = 1e-06
grad_eps = 1e-06
reg_weight = 0.3
step_rate = 0.25
error_scale = 600.0


def exchange(x, axes):
    return lax.all_to_all(x, axes, 0, 0, tiled=True)


def total_over(x, axes):
    peers = 1
    for axis in axes if isinstance(axes, tuple) else (axes,):
        peers *= lax.axis_size(axis)
    return jnp.sum(exchange(jnp.broadcast_to(x[None], (peers, *x.shape)), axes), axis=0)


def unpack(words):
    shifts = 3 * jnp.arange(4, dtype=jnp.int32)
    codes = jnp.right_shift(words[:, None, :], shifts[None, :, None]) & 7
    return codes.reshape(words.shape[0] * 4, words.shape[1]).astype(jnp.float32) - 4.0


def soft_round(values):
    sig = jax.nn.sigmoid(values)
    linear = 1.2 * sig - 0.1
    soft_part = jnp.clip(linear, 0.0, 1.0)
    soft_slope = jnp.where((linear > 0.0) & (linear < 1.0), 1.2 * sig * (1.0 - sig), 0.0)
    return (soft_part, soft_slope)


def per_device(activations, targets, packed_floors, rounding, scales, norm_gains):
    sections = lax.axis_size("section")
    dps = lax.axis_size("dp")
    tensors = lax.axis_size("tensor_0") * lax.axis_size("tensor_1")
    section_index = lax.axis_index("section")
    dp_index = lax.axis_index("dp")
    tok_dev, width_local = activations.shape
    width_full = norm_gains.shape[1]
    token_total = tok_dev * dps
    rows_local = width_full // dps
    near = tensors // dps
    own = width_local // dps
    tok_part = tok_dev // sections
    tok_group = tok_part * dps
    soft_part, soft_slope = soft_round(rounding[0])
    channel_scale = scales[0][None, :]
    weight = (channel_scale * (unpack(packed_floors[0]) + soft_part)).astype(jnp.bfloat16)
    weight = weight.reshape(near, dps, own, width_local).transpose(1, 0, 2, 3)
    weight = exchange(weight.reshape(dps, near * own, width_local), "dp")
    weights = lax.all_gather(weight.reshape(rows_local, width_local), "section", axis=0)
    gains_own = norm_gains[0].reshape(tensors, dps, own)
    gains_own = lax.dynamic_index_in_dim(gains_own, dp_index, 1, keepdims=False).reshape(
        1, rows_local
    )
    gains = lax.all_gather(gains_own, "section", axis=0, tiled=True)
    fresh = lax.dynamic_slice_in_dim(activations, section_index * tok_part, tok_part, 0)
    fresh = exchange(fresh.reshape(tok_part, dps, own).transpose(1, 0, 2), "dp")
    current = fresh.reshape(tok_group, own).T
    target_all = lax.all_gather(targets[0], "dp", axis=0)
    target_all = target_all.reshape(dps, sections, tok_part, width_local).transpose(1, 0, 2, 3)
    target_all = target_all.reshape(token_total, width_local).astype(jnp.float32)
    sent = []
    for block in range(sections):
        features = lax.all_gather(current, TENSOR, axis=0, tiled=True).astype(jnp.float32)
        gain = gains[block][:, None]
        scaled = (features * gain).astype(jnp.bfloat16)
        partial = lax.dot_general(
            weights[block], scaled, (((0,), (0,)), ((), ())), preferred_element_type=jnp.float32
        )
        squares = jnp.sum(features * features, axis=0)
        piece = jnp.concatenate(
            [
                partial.reshape(dps, own, tok_group),
                jnp.broadcast_to(squares[None, None], (dps, 8, tok_group)),
            ],
            axis=1,
        )
        summed = jnp.sum(exchange(piece, "dp"), axis=0)
        rate = lax.rsqrt(summed[own : own + 1] / width_full + norm_eps)
        current = (current.astype(jnp.float32) + rate * summed[:own]).astype(jnp.bfloat16)
        normed = (features * rate * gain).astype(jnp.bfloat16)
        sent.append(
            jnp.concatenate(
                [
                    normed.reshape(dps, near * own, tok_group),
                    jnp.broadcast_to(current[None], (dps, own, tok_group)),
                ],
                axis=1,
            )
        )
    came = exchange(jnp.concatenate(sent, axis=0), PLANE)
    came = came.reshape(sections, dps, near * own + own, tok_group)
    rows = came[:, :, : near * own].reshape(sections, dps, near, own, tok_group)
    rows = rows.transpose(2, 1, 3, 0, 4).reshape(rows_local, token_total)
    result = came[:, :, near * own :].transpose(0, 3, 1, 2).reshape(token_total, width_local)
    residue = result.astype(jnp.float32) - target_all
    delta = (error_scale / token_total**0.5 * residue).astype(jnp.bfloat16)
    grad_w = jnp.dot(rows, delta, preferred_element_type=jnp.float32)
    polarity = 2.0 * soft_part - 1.0
    grad = soft_slope * (channel_scale * grad_w - 8.0 * reg_weight * polarity**3)
    sums = jnp.stack(
        [jnp.sum(residue * residue) / dps, jnp.sum(1.0 - polarity**4), jnp.sum(grad * grad)]
    )
    sums = jnp.broadcast_to(jnp.pad(sums, (0, 5))[:, None], (8, 128))
    sums = total_over(total_over(sums, TENSOR), "dp")[:, 0]
    mean_grad = sums[2] / (width_full * width_full) + grad_eps
    rounding_next = rounding[0] - step_rate * grad * lax.rsqrt(mean_grad)
    loss_value = sums[0] / (token_total * width_full) + reg_weight * sums[1] / (
        width_full * width_full
    )
    outputs = lax.dynamic_index_in_dim(
        result.reshape(sections, dps, tok_part, width_local), dp_index, 1, keepdims=False
    )
    return (rounding_next[None], outputs.reshape(1, tok_dev, width_local), loss_value.reshape(1))


def solution(mesh):
    torus = Mesh(
        mesh.devices.reshape(mesh.shape["section"], mesh.shape["dp"], 16, 2),
        ("section", "dp", "tensor_0", "tensor_1"),
    )
    return jax.shard_map(
        per_device,
        mesh=torus,
        in_specs=(
            P("dp", TENSOR),
            P("section", "dp", TENSOR),
            P("section", "dp", TENSOR),
            P("section", "dp", TENSOR),
            P("section", TENSOR),
            P("section", None),
        ),
        out_specs=(P("section", "dp", TENSOR), P("section", "dp", TENSOR), P("section")),
        check_vma=False,
    )
```

profile of v0, /device:TPU:4, one launch (start us, length us, event | category | flops | bytes accessed | tf_op | source)
XLA Modules:
  0.0 358.8 jit_solution(6779789227103633169)
XLA Ops:
  7.2 2.7 shift_right_arithmetic.24
  10.0 3.1 shift_right_arithmetic.25
  13.1 1.9 add_clamp_fusion
  15.1 2.8 fusion.27
  18.0 19.5 %all_to_all.45 = bf16[4,512,256]{2,1,0:T(8,128)(2,1)} all-to-all(bf16[4,512,256]{2,1,0:T(8,128)(2,1)S(1)} %bitcast.124), channel_id=1, replica_groups=mesh['section'=4,'dp'=4,'tensor_0'=16,'tensor_1'=2] {'dp'}, dimensions={0} | all-to-all | bytes 2097152 | tf_op jit(solution)/shard_map/all_to_all | solution.py:17
  38.3 3.3 all-to-all-start
  43.0 10.7 %all-gather = f32[4,1,2048]{2,1,0:T(1,128)S(1)} all-gather(f32[1,1,2048]{2,1,0:T(1,128)S(1)} %reshape.147), channel_id=1, replica_groups=mesh['section'=4,'dp'=4,'tensor_0'=16,'tensor_1'=2] {'section'}, dimensions={0}, use_global_device_ids=true | all-gather | bytes 40960 | tf_op jit(solution)/shard_map/all_gather | solution.py:65
  53.9 37.7 %all_gather.21 = bf16[2048,128]{1,0:T(8,128)(2,1)S(1)} all-gather(bf16[64,128]{1,0:T(8,128)(2,1)S(1)} %bitcast.137), channel_id=1, replica_groups=mesh['section'=4,'dp'=4,'tensor_0'=16,'tensor_1'=2] {'tensor_0','tensor_1'}, dimensions={0}, use_global_device_ids=true | all-gather | bytes 540672 | tf_op jit(solution)/shard_map/all_gather | solution.py:74
  91.8 3.2 all-gather.3.cloned.1.call-done
  95.0 4.3 %slice_bitcast_fusion = (bf16[256,2048]{0,1:T(8,128)(2,1)}, bf16[256,2048]{0,1:T(8,128)(2,1)}, bf16[256,2048]{0,1:T(8,128)(2,1)}, bf16[256,2048]{0,1:T(8,128)(2,1)}) fusion(bf16[4,2048,256]{2,1,0:T(8,128)(2,1)} %all-gather.3.cloned.1.call-done), kind=kLoop, calls=%fused_computation.50 | loop fusion | bytes 8388608 | tf_op jit(solution)/shard_map/dot_general | solution.py:77
  99.3 2.3 copy.54
  101.6 1.8 fusion.38
  104.0 4.3 %all-to-all-start.2 = ((f32[4,72,128]{2,1,0:T(8,128)}), f32[4,72,128]{2,1,0:T(8,128)S(1)}, u32[]{:S(2)}, u32[]{:S(2)}) async-start(f32[4,72,128]{2,1,0:T(8,128)} %pad_maximum_fusion), calls=%async_computation.2 | async-start | bytes 294912 | tf_op jit(solution)/shard_map/all_to_all | solution.py:17
  108.3 2.3 copy.56
  110.6 2.3 copy.57
  112.9 2.3 copy.58
  115.2 32.4 %all_gather.24 = bf16[2048,128]{1,0:T(8,128)(2,1)S(1)} all-gather(bf16[64,128]{1,0:T(8,128)(2,1)S(1)} %fusion.53), channel_id=1, replica_groups=mesh['section'=4,'dp'=4,'tensor_0'=16,'tensor_1'=2] {'tensor_0','tensor_1'}, dimensions={0}, use_global_device_ids=true | all-gather | bytes 540672 | tf_op jit(solution)/shard_map/all_gather | solution.py:74
  147.9 1.8 fusion.35
  150.4 4.8 %all-to-all-start.3 = ((f32[4,72,128]{2,1,0:T(8,128)}), f32[4,72,128]{2,1,0:T(8,128)S(1)}, u32[]{:S(2)}, u32[]{:S(2)}) async-start(f32[4,72,128]{2,1,0:T(8,128)} %pad_maximum_fusion.1), calls=%async_computation.3 | async-start | bytes 294912 | tf_op jit(solution)/shard_map/all_to_all | solution.py:17
  155.2 1.1 fusion.14
  156.3 4.9 %all-to-all-done.3 = f32[4,72,128]{2,1,0:T(8,128)S(1)} async-done(((f32[4,72,128]{2,1,0:T(8,128)}), f32[4,72,128]{2,1,0:T(8,128)S(1)}, u32[]{:S(2)}, u32[]{:S(2)}) %all-to-all-start.3) | async-done | bytes 147488 | tf_op jit(solution)/shard_map/all_to_all | solution.py:17
  161.3 29.5 %all_gather.25 = bf16[2048,128]{1,0:T(8,128)(2,1)S(1)} all-gather(bf16[64,128]{1,0:T(8,128)(2,1)S(1)} %fusion.51), channel_id=1, replica_groups=mesh['section'=4,'dp'=4,'tensor_0'=16,'tensor_1'=2] {'tensor_0','tensor_1'}, dimensions={0}, use_global_device_ids=true | all-gather | bytes 540672 | tf_op jit(solution)/shard_map/all_gather | solution.py:74
  191.1 1.8 fusion.32
  193.6 3.3 all-to-all-start.4
  196.9 1.1 fusion.18
  198.1 5.0 %all-to-all-done.4 = f32[4,72,128]{2,1,0:T(8,128)S(1)} async-done(((f32[4,72,128]{2,1,0:T(8,128)}), f32[4,72,128]{2,1,0:T(8,128)S(1)}, u32[]{:S(2)}, u32[]{:S(2)}) %all-to-all-start.4) | async-done | bytes 147488 | tf_op jit(solution)/shard_map/all_to_all | solution.py:17
  203.2 30.0 %all_gather.26 = bf16[2048,128]{1,0:T(8,128)(2,1)S(1)} all-gather(bf16[64,128]{1,0:T(8,128)(2,1)S(1)} %fusion.49), channel_id=1, replica_groups=mesh['section'=4,'dp'=4,'tensor_0'=16,'tensor_1'=2] {'tensor_0','tensor_1'}, dimensions={0}, use_global_device_ids=true | all-gather | bytes 540672 | tf_op jit(solution)/shard_map/all_gather | solution.py:74
  233.5 1.8 fusion.29
  236.0 3.5 all-to-all-start.5
  239.5 1.1 fusion.22
  240.6 4.9 %all-to-all-done.5 = f32[4,72,128]{2,1,0:T(8,128)S(1)} async-done(((f32[4,72,128]{2,1,0:T(8,128)}), f32[4,72,128]{2,1,0:T(8,128)S(1)}, u32[]{:S(2)}, u32[]{:S(2)}) %all-to-all-start.5) | async-done | bytes 147488 | tf_op jit(solution)/shard_map/all_to_all | solution.py:17
  245.9 6.8 %maximum_maximum_fusion = bf16[16,576,128]{2,1,0:T(8,128)(2,1)} fusion(bf16[4,64,128]{2,1,0:T(8,128)(2,1)S(1)} %broadcast_in_dim.29, bf16[4,512,128]{2,1,0:T(8,128)(2,1)S(1)} %bitcast.128, bf16[4,64,128]{2,1,0:T(8,128)(2,1)S(1)} %broadcast_in_dim.27, bf16[4,512,128]{2,1,0:T(8,128)(2,1)} %bitcast.127, bf16[4,64,128]{2,1,0:T(8,128)(2,1)S(1)} %broadcast_in_dim.25, ...), kind=kLoop, calls=%fused_computation.5 | loop fusion | flops 18874368 | bytes 4718592 | tf_op jit(solution)/shard_map/concatenate | solution.py:101
  252.8 5.8 %all-to-all-start.6 = ((bf16[16,576,128]{2,1,0:T(8,128)(2,1)}), bf16[16,576,128]{2,1,0:T(8,128)(2,1)}, u32[]{:S(2)}, u32[]{:S(2)}) async-start(bf16[16,576,128]{2,1,0:T(8,128)(2,1)} %maximum_maximum_fusion), calls=%async_computation.6 | async-start | bytes 4718592 | tf_op jit(solution)/shard_map/all_to_all | solution.py:17
  258.6 35.7 %all_gather.27 = bf16[4,128,256]{2,1,0:T(8,128)(2,1)S(1)} all-gather(bf16[1,128,256]{2,1,0:T(8,128)(2,1)S(1)} %copy-done.3), channel_id=1, replica_groups=mesh['section'=4,'dp'=4,'tensor_0'=16,'tensor_1'=2] {'dp'}, dimensions={0}, use_global_device_ids=true | all-gather | bytes 327680 | tf_op jit(solution)/shard_map/all_gather | solution.py:69
  295.1 1.5 reshape.140
  296.6 1.1 copy.61
  297.7 1.5 fusion.4
  299.2 1.7 slice.111
  301.0 2.0 copy.59
  303.0 1.7 multiply_reduce_fusion.1
  304.9 3.9 %multiply_reduce_fusion = (f32[]{:T(128)}, f32[2048,256]{1,0:T(8,128)}) fusion(bf16[32,8,4,128]{3,2,1,0:T(4,128)(2,1)S(1)} %bitcast.136, bf16[256,8,4,128]{3,2,1,0:T(4,128)(2,1)S(1)} %bitcast.129, f32[256]{0:T(256)S(1)} %bitcast.151, f32[1,2048,256]{2,1,0:T(8,128)S(1)} %copy-done.1), kind=kOutput, calls=%fused_computation.18 | convolution fusion | flops 548405248 | bytes 6554628 | tf_op jit(solution)/shard_map/dot_general | solution.py:108
  309.4 1.3 select_maximum_fusion
  311.4 7.3 %all-to-all-start.7 = ((f32[32,8,128]{2,1,0:T(8,128)}), f32[32,8,128]{2,1,0:T(8,128)S(1)}, u32[]{:S(2)}, u32[]{:S(2)}) async-start(f32[32,8,128]{2,1,0:T(8,128)} %broadcast_in_dim_broadcast_in_dim_broadcast_in_dim.2), calls=%async_computation.7 | async-start | bytes 262144 | tf_op jit(solution)/shard_map/all_to_all | solution.py:17
  318.7 1.0 slice_bitcast_fusion.4
  320.3 15.6 %all-to-all-done.7 = f32[32,8,128]{2,1,0:T(8,128)S(1)} async-done(((f32[32,8,128]{2,1,0:T(8,128)}), f32[32,8,128]{2,1,0:T(8,128)S(1)}, u32[]{:S(2)}, u32[]{:S(2)}) %all-to-all-start.7) | async-done | bytes 131104 | tf_op jit(solution)/shard_map/all_to_all | solution.py:17
  336.6 3.2 all-to-all-start.8
  340.5 4.7 %all-to-all-done.8 = f32[4,8,128]{2,1,0:T(8,128)S(1)} async-done(((f32[4,8,128]{2,1,0:T(8,128)}), f32[4,8,128]{2,1,0:T(8,128)S(1)}, u32[]{:S(2)}, u32[]{:S(2)}) %all-to-all-start.8) | async-done | bytes 16416 | tf_op jit(solution)/shard_map/all_to_all | solution.py:17
  347.7 3.2 fusion.10
  (72 shorter events, 11.3 us)
Async XLA Ops:
  7.2 30.3 %copy-start = (bf16[128,256]{1,0:T(8,128)(2,1)S(1)}, bf16[128,256]{1,0:T(8,128)(2,1)}, u32[]{:S(2)}) copy-start(bf16[128,256]{1,0:T(8,128)(2,1)} %param.6) | copy-start | bytes 196612
  7.2 87.8 %all-gather.3.cloned.1.call-start = ((), (), s32[]{:S(2)}) async-start(), calls=%async_computation.9 | async-start | bytes 5242880 | tf_op jit(solution)/shard_map/all_gather | solution.py:60
  10.0 3.1 copy-start.1
  13.1 2.0 copy-start.5
  18.0 24.1 %copy-start.4 = (f32[1,8192]{1,0:T(1,128)S(1)}, f32[1,8192]{1,0:T(1,128)}, u32[]{:S(2)}) copy-start(f32[1,8192]{1,0:T(1,128)} %param.11) | copy-start | bytes 98308
  38.3 15.4 %all-to-all-start = ((bf16[4,2,1024]{2,1,0:T(2,128)(2,1)}), bf16[4,2,1024]{2,1,0:T(2,128)(2,1)S(1)}, u32[]{:S(2)}, u32[]{:S(2)}) async-start(bf16[4,2,1024]{2,1,0:T(2,128)(2,1)} %reshape.171), calls=%async_computation | async-start | bytes 32768 | tf_op jit(solution)/shard_map/all_to_all | solution.py:17
  104.0 11.1 %all-to-all-start.2 = ((f32[4,72,128]{2,1,0:T(8,128)}), f32[4,72,128]{2,1,0:T(8,128)S(1)}, u32[]{:S(2)}, u32[]{:S(2)}) async-start(f32[4,72,128]{2,1,0:T(8,128)} %pad_maximum_fusion), calls=%async_computation.2 | async-start | bytes 294912 | tf_op jit(solution)/shard_map/all_to_all | solution.py:17
  150.4 10.9 %all-to-all-start.3 = ((f32[4,72,128]{2,1,0:T(8,128)}), f32[4,72,128]{2,1,0:T(8,128)S(1)}, u32[]{:S(2)}, u32[]{:S(2)}) async-start(f32[4,72,128]{2,1,0:T(8,128)} %pad_maximum_fusion.1), calls=%async_computation.3 | async-start | bytes 294912 | tf_op jit(solution)/shard_map/all_to_all | solution.py:17
  193.6 9.5 %all-to-all-start.4 = ((f32[4,72,128]{2,1,0:T(8,128)}), f32[4,72,128]{2,1,0:T(8,128)S(1)}, u32[]{:S(2)}, u32[]{:S(2)}) async-start(f32[4,72,128]{2,1,0:T(8,128)} %pad_maximum_fusion.2), calls=%async_computation.4 | async-start | bytes 294912 | tf_op jit(solution)/shard_map/all_to_all | solution.py:17
  236.0 9.5 %all-to-all-start.5 = ((f32[4,72,128]{2,1,0:T(8,128)}), f32[4,72,128]{2,1,0:T(8,128)S(1)}, u32[]{:S(2)}, u32[]{:S(2)}) async-start(f32[4,72,128]{2,1,0:T(8,128)} %pad_maximum_fusion.3), calls=%async_computation.5 | async-start | bytes 294912 | tf_op jit(solution)/shard_map/all_to_all | solution.py:17
  252.8 5.8 %copy-start.3 = (bf16[1,128,256]{2,1,0:T(8,128)(2,1)S(1)}, bf16[1,128,256]{2,1,0:T(8,128)(2,1)}, u32[]{:S(2)}) copy-start(bf16[1,128,256]{2,1,0:T(8,128)(2,1)} %param.7) | copy-start | bytes 196612
  252.8 46.4 %all-to-all-start.6 = ((bf16[16,576,128]{2,1,0:T(8,128)(2,1)}), bf16[16,576,128]{2,1,0:T(8,128)(2,1)}, u32[]{:S(2)}, u32[]{:S(2)}) async-start(bf16[16,576,128]{2,1,0:T(8,128)(2,1)} %maximum_maximum_fusion), calls=%async_computation.6 | async-start | bytes 4718592 | tf_op jit(solution)/shard_map/all_to_all | solution.py:17
  301.0 2.0 copy-start.2
  311.4 24.5 %all-to-all-start.7 = ((f32[32,8,128]{2,1,0:T(8,128)}), f32[32,8,128]{2,1,0:T(8,128)S(1)}, u32[]{:S(2)}, u32[]{:S(2)}) async-start(f32[32,8,128]{2,1,0:T(8,128)} %broadcast_in_dim_broadcast_in_dim_broadcast_in_dim.2), calls=%async_computation.7 | async-start | bytes 262144 | tf_op jit(solution)/shard_map/all_to_all | solution.py:17
  336.6 8.6 %all-to-all-start.8 = ((f32[4,8,128]{2,1,0:T(8,128)}), f32[4,8,128]{2,1,0:T(8,128)S(1)}, u32[]{:S(2)}, u32[]{:S(2)}) async-start(f32[4,8,128]{2,1,0:T(8,128)} %broadcast_in_dim.30), calls=%async_computation.8 | async-start | bytes 32768 | tf_op jit(solution)/shard_map/all_to_all | solution.py:17
Sparse Core Ops, SparseCore 0:
  37.6 57.3 all-gather.2
where the time goes:
time: 360 us; the launch traced here: 359 us
  blocking collectives  196 us (54%)
  waiting for transfers between devices  38.3 us (11%)
  starting transfers between devices  35.6 us (10%)
  local copies, waits for them, and re-layouts  31.9 us (9%)
  other arithmetic  28.4 us (8%)
  between operations  18.2 us (5%)
  matrix products  11 us (3%)
    all_gather x4, blocking collectives, per_device(): lax.all_gather(current, TENSOR, axis=0, tiled=True).astype(jnp.float32)  130 us
    all_gather x1, blocking collectives, per_device(): target_all = lax.all_gather(targets[0], 'dp', axis=0)  35.7 us
    all_to_all x8, starting transfers between devices, exchange(): return lax.all_to_all(x, axes, 0, 0, tiled=True)  35.5 us
    all_to_all x8, waiting for transfers between devices, exchange(): return lax.all_to_all(x, axes, 0, 0, tiled=True)  35.1 us
    all_to_all x1, blocking collectives, exchange(): return lax.all_to_all(x, axes, 0, 0, tiled=True)  19.5 us
    dot_general x5, local copies, waits for them, and re-layouts, per_device(): lax.dot_general(weights[block], scaled, (((0,), (0,)), ((), ())), preferr...  13.4 us
    all_gather x1, blocking collectives, per_device(): gains = lax.all_gather(gains_own, 'section', axis=0, tiled=True)  10.7 us
  transfers between devices with their start and end apart: 9, of which 6 were waited for; matrix products, arithmetic and copies ran while one was open for 6% of the time, Pallas kernels for 0%

commit v1 on v0

--- a/solution.py
+++ b/solution.py
@@ -62,7 +62,9 @@
     gains_own = lax.dynamic_index_in_dim(gains_own, dp_index, 1, keepdims=False).reshape(
         1, rows_local
     )
-    gains = lax.all_gather(gains_own, "section", axis=0, tiled=True)
+    gains = jnp.concatenate(
+        lax.all_to_all(jnp.stack([gains_own] * lax.axis_size("section")), "section", 0, 0), axis=0
+    )
     fresh = lax.dynamic_slice_in_dim(activations, section_index * tok_part, tok_part, 0)
     fresh = exchange(fresh.reshape(tok_part, dps, own).transpose(1, 0, 2), "dp")
     current = fresh.reshape(tok_group, own).T

time: 360 us -> 360 us (level)
  blocking collectives: 196 us -> 185 us
  waiting for transfers between devices: 38.3 us -> 43.5 us
  starting transfers between devices: 35.6 us -> 40.4 us
    all_gather x1 -> x0, blocking collectives: 10.7 us -> none  [per_device(): gains = lax.all_gather(gains_own, 'section', axis=0, tiled=True)]
    all_to_all x0 -> x1, starting transfers between devices: none -> 4.8 us  [per_device(): lax.all_to_all(jnp.stack([gains_own] * lax.axis_size('section')), 'sectio...]
    all_to_all x8, waiting for transfers between devices: 35.1 us -> 39 us  [exchange(): return lax.all_to_all(x, axes, 0, 0, tiled=True)]
  transfers between devices with their start and end apart: 9 -> 10, of which waited for: 6 -> 7; matrix products, arithmetic and copies ran while one was open for 6% -> 6% of each run, Pallas kernels for 0% -> 0%
where the time goes in v1:
time: 360 us; the launch traced here: 359 us
  blocking collectives  185 us (51%)
  waiting for transfers between devices  43.5 us (12%)
  starting transfers between devices  40.4 us (11%)
  local copies, waits for them, and re-layouts  32.6 us (9%)
  other arithmetic  28.4 us (8%)
  between operations  18.2 us (5%)
  matrix products  11 us (3%)
    all_gather x4, blocking collectives, per_device(): lax.all_gather(current, TENSOR, axis=0, tiled=True).astype(jnp.float32)  130 us
    all_to_all x8, waiting for transfers between devices, exchange(): return lax.all_to_all(x, axes, 0, 0, tiled=True)  39 us
    all_gather x1, blocking collectives, per_device(): target_all = lax.all_gather(targets[0], 'dp', axis=0)  35.7 us
    all_to_all x8, starting transfers between devices, exchange(): return lax.all_to_all(x, axes, 0, 0, tiled=True)  35.5 us
    all_to_all x1, blocking collectives, exchange(): return lax.all_to_all(x, axes, 0, 0, tiled=True)  19.5 us
    dot_general x5, local copies, waits for them, and re-layouts, per_device(): lax.dot_general(weights[block], scaled, (((0,), (0,)), ((), ())), preferr...  13.4 us
  transfers between devices with their start and end apart: 10, of which 7 were waited for; matrix products, arithmetic and copies ran while one was open for 6% of the time, Pallas kernels for 0%

profile of v1, /device:TPU:4, one launch (start us, length us, event | category | flops | bytes accessed | tf_op | source)
XLA Modules:
  0.0 358.8 jit_solution(8259019507140550224)
XLA Ops:
  7.2 2.7 shift_right_arithmetic.24
  10.0 3.1 shift_right_arithmetic.25
  13.1 1.9 add_clamp_fusion
  15.1 2.8 fusion.27
  18.0 19.5 %all_to_all.50 = bf16[4,512,256]{2,1,0:T(8,128)(2,1)} all-to-all(bf16[4,512,256]{2,1,0:T(8,128)(2,1)S(1)} %bitcast.121), channel_id=1, replica_groups=mesh['section'=4,'dp'=4,'tensor_0'=16,'tensor_1'=2] {'dp'}, dimensions={0} | all-to-all | bytes 2097152 | tf_op jit(solution)/shard_map/all_to_all | solution.py:17
  38.3 3.3 all-to-all-start
  43.0 3.8 %all-to-all-done = bf16[4,2,1024]{2,1,0:T(2,128)(2,1)S(1)} async-done(((bf16[4,2,1024]{2,1,0:T(2,128)(2,1)}), bf16[4,2,1024]{2,1,0:T(2,128)(2,1)S(1)}, u32[]{:S(2)}, u32[]{:S(2)}) %all-to-all-start) | async-done | bytes 16416 | tf_op jit(solution)/shard_map/all_to_all | solution.py:17
  47.5 4.8 %all-to-all-start.2 = ((f32[4,1,2048]{2,1,0:T(1,128)}), f32[4,1,2048]{2,1,0:T(1,128)S(1)}, u32[]{:S(2)}, u32[]{:S(2)}) async-start(f32[4,1,2048]{2,1,0:T(1,128)} %stack.15), calls=%async_computation.2 | async-start | bytes 65536 | tf_op jit(solution)/shard_map/all_to_all | solution.py:66
  52.5 37.7 %all_gather.18 = bf16[2048,128]{1,0:T(8,128)(2,1)S(1)} all-gather(bf16[64,128]{1,0:T(8,128)(2,1)S(1)} %bitcast.134), channel_id=1, replica_groups=mesh['section'=4,'dp'=4,'tensor_0'=16,'tensor_1'=2] {'tensor_0','tensor_1'}, dimensions={0}, use_global_device_ids=true | all-gather | bytes 540672 | tf_op jit(solution)/shard_map/all_gather | solution.py:76
  90.5 4.5 %all-gather.2.cloned.1.call-done = bf16[4,2048,256]{2,1,0:T(8,128)(2,1)} async-done(((bf16[1,2048,256]{2,1,0:T(8,128)(2,1)}), bf16[4,2048,256]{2,1,0:T(8,128)(2,1)}) %all-gather.2.cloned.1.call-update) | async-done | bytes 4194320 | tf_op jit(solution)/shard_map/all_gather | solution.py:60
  95.0 4.3 %slice_bitcast_fusion = (bf16[256,2048]{0,1:T(8,128)(2,1)}, bf16[256,2048]{0,1:T(8,128)(2,1)}, bf16[256,2048]{0,1:T(8,128)(2,1)}, bf16[256,2048]{0,1:T(8,128)(2,1)}) fusion(bf16[4,2048,256]{2,1,0:T(8,128)(2,1)} %all-gather.2.cloned.1.call-done), kind=kLoop, calls=%fused_computation.50 | loop fusion | bytes 8388608 | tf_op jit(solution)/shard_map/dot_general | solution.py:79
  99.3 2.3 copy.53
  101.6 1.8 fusion.38
  104.0 4.3 %all-to-all-start.3 = ((f32[4,72,128]{2,1,0:T(8,128)}), f32[4,72,128]{2,1,0:T(8,128)S(1)}, u32[]{:S(2)}, u32[]{:S(2)}) async-start(f32[4,72,128]{2,1,0:T(8,128)} %pad_maximum_fusion), calls=%async_computation.3 | async-start | bytes 294912 | tf_op jit(solution)/shard_map/all_to_all | solution.py:17
  108.3 2.3 copy.54
  110.6 2.3 copy.55
  112.9 2.3 copy.56
  115.2 32.4 %all_gather.20 = bf16[2048,128]{1,0:T(8,128)(2,1)S(1)} all-gather(bf16[64,128]{1,0:T(8,128)(2,1)S(1)} %fusion.53), channel_id=1, replica_groups=mesh['section'=4,'dp'=4,'tensor_0'=16,'tensor_1'=2] {'tensor_0','tensor_1'}, dimensions={0}, use_global_device_ids=true | all-gather | bytes 540672 | tf_op jit(solution)/shard_map/all_gather | solution.py:76
  147.9 1.8 fusion.35
  150.4 4.8 %all-to-all-start.4 = ((f32[4,72,128]{2,1,0:T(8,128)}), f32[4,72,128]{2,1,0:T(8,128)S(1)}, u32[]{:S(2)}, u32[]{:S(2)}) async-start(f32[4,72,128]{2,1,0:T(8,128)} %pad_maximum_fusion.1), calls=%async_computation.4 | async-start | bytes 294912 | tf_op jit(solution)/shard_map/all_to_all | solution.py:17
  155.2 1.1 fusion.14
  156.3 4.9 %all-to-all-done.4 = f32[4,72,128]{2,1,0:T(8,128)S(1)} async-done(((f32[4,72,128]{2,1,0:T(8,128)}), f32[4,72,128]{2,1,0:T(8,128)S(1)}, u32[]{:S(2)}, u32[]{:S(2)}) %all-to-all-start.4) | async-done | bytes 147488 | tf_op jit(solution)/shard_map/all_to_all | solution.py:17
  161.3 29.5 %all_gather.21 = bf16[2048,128]{1,0:T(8,128)(2,1)S(1)} all-gather(bf16[64,128]{1,0:T(8,128)(2,1)S(1)} %fusion.51), channel_id=1, replica_groups=mesh['section'=4,'dp'=4,'tensor_0'=16,'tensor_1'=2] {'tensor_0','tensor_1'}, dimensions={0}, use_global_device_ids=true | all-gather | bytes 540672 | tf_op jit(solution)/shard_map/all_gather | solution.py:76
  191.1 1.8 fusion.32
  193.6 3.3 all-to-all-start.5
  196.9 1.1 fusion.18
  198.1 5.0 %all-to-all-done.5 = f32[4,72,128]{2,1,0:T(8,128)S(1)} async-done(((f32[4,72,128]{2,1,0:T(8,128)}), f32[4,72,128]{2,1,0:T(8,128)S(1)}, u32[]{:S(2)}, u32[]{:S(2)}) %all-to-all-start.5) | async-done | bytes 147488 | tf_op jit(solution)/shard_map/all_to_all | solution.py:17
  203.2 30.0 %all_gather.22 = bf16[2048,128]{1,0:T(8,128)(2,1)S(1)} all-gather(bf16[64,128]{1,0:T(8,128)(2,1)S(1)} %fusion.49), channel_id=1, replica_groups=mesh['section'=4,'dp'=4,'tensor_0'=16,'tensor_1'=2] {'tensor_0','tensor_1'}, dimensions={0}, use_global_device_ids=true | all-gather | bytes 540672 | tf_op jit(solution)/shard_map/all_gather | solution.py:76
  233.5 1.8 fusion.29
  236.0 3.5 all-to-all-start.6
  239.5 1.1 fusion.22
  240.6 4.9 %all-to-all-done.6 = f32[4,72,128]{2,1,0:T(8,128)S(1)} async-done(((f32[4,72,128]{2,1,0:T(8,128)}), f32[4,72,128]{2,1,0:T(8,128)S(1)}, u32[]{:S(2)}, u32[]{:S(2)}) %all-to-all-start.6) | async-done | bytes 147488 | tf_op jit(solution)/shard_map/all_to_all | solution.py:17
  245.9 6.8 %maximum_maximum_fusion = bf16[16,576,128]{2,1,0:T(8,128)(2,1)} fusion(bf16[4,64,128]{2,1,0:T(8,128)(2,1)S(1)} %broadcast_in_dim.29, bf16[4,512,128]{2,1,0:T(8,128)(2,1)S(1)} %bitcast.125, bf16[4,64,128]{2,1,0:T(8,128)(2,1)S(1)} %broadcast_in_dim.27, bf16[4,512,128]{2,1,0:T(8,128)(2,1)} %bitcast.124, bf16[4,64,128]{2,1,0:T(8,128)(2,1)S(1)} %broadcast_in_dim.25, ...), kind=kLoop, calls=%fused_computation.5 | loop fusion | flops 18874368 | bytes 4718592 | tf_op jit(solution)/shard_map/concatenate | solution.py:103
  252.8 5.8 %all-to-all-start.7 = ((bf16[16,576,128]{2,1,0:T(8,128)(2,1)}), bf16[16,576,128]{2,1,0:T(8,128)(2,1)}, u32[]{:S(2)}, u32[]{:S(2)}) async-start(bf16[16,576,128]{2,1,0:T(8,128)(2,1)} %maximum_maximum_fusion), calls=%async_computation.7 | async-start | bytes 4718592 | tf_op jit(solution)/shard_map/all_to_all | solution.py:17
  258.6 35.7 %all_gather.23 = bf16[4,128,256]{2,1,0:T(8,128)(2,1)S(1)} all-gather(bf16[1,128,256]{2,1,0:T(8,128)(2,1)S(1)} %copy-done.3), channel_id=1, replica_groups=mesh['section'=4,'dp'=4,'tensor_0'=16,'tensor_1'=2] {'dp'}, dimensions={0}, use_global_device_ids=true | all-gather | bytes 327680 | tf_op jit(solution)/shard_map/all_gather | solution.py:71
  295.1 1.5 reshape.149
  296.6 1.1 copy.59
  297.7 1.5 fusion.4
  299.2 1.7 slice.111
  301.0 2.0 copy.57
  303.0 1.7 multiply_reduce_fusion.1
  304.9 3.9 %multiply_reduce_fusion = (f32[]{:T(128)}, f32[2048,256]{1,0:T(8,128)}) fusion(bf16[32,8,4,128]{3,2,1,0:T(4,128)(2,1)S(1)} %bitcast.133, bf16[256,8,4,128]{3,2,1,0:T(4,128)(2,1)S(1)} %bitcast.126, f32[256]{0:T(256)S(1)} %bitcast.147, f32[1,2048,256]{2,1,0:T(8,128)S(1)} %copy-done.1), kind=kOutput, calls=%fused_computation.18 | convolution fusion | flops 548405248 | bytes 6554628 | tf_op jit(solution)/shard_map/dot_general | solution.py:110
  309.4 1.3 select_maximum_fusion
  311.4 7.3 %all-to-all-start.8 = ((f32[32,8,128]{2,1,0:T(8,128)}), f32[32,8,128]{2,1,0:T(8,128)S(1)}, u32[]{:S(2)}, u32[]{:S(2)}) async-start(f32[32,8,128]{2,1,0:T(8,128)} %broadcast_in_dim_broadcast_in_dim_broadcast_in_dim.2), calls=%async_computation.8 | async-start | bytes 262144 | tf_op jit(solution)/shard_map/all_to_all | solution.py:17
  320.3 15.6 %all-to-all-done.8 = f32[32,8,128]{2,1,0:T(8,128)S(1)} async-done(((f32[32,8,128]{2,1,0:T(8,128)}), f32[32,8,128]{2,1,0:T(8,128)S(1)}, u32[]{:S(2)}, u32[]{:S(2)}) %all-to-all-start.8) | async-done | bytes 131104 | tf_op jit(solution)/shard_map/all_to_all | solution.py:17
  336.6 3.2 all-to-all-start.9
  340.5 4.7 %all-to-all-done.9 = f32[4,8,128]{2,1,0:T(8,128)S(1)} async-done(((f32[4,8,128]{2,1,0:T(8,128)}), f32[4,8,128]{2,1,0:T(8,128)S(1)}, u32[]{:S(2)}, u32[]{:S(2)}) %all-to-all-start.9) | async-done | bytes 16416 | tf_op jit(solution)/shard_map/all_to_all | solution.py:17
  347.7 3.2 fusion.10
  (74 shorter events, 12.9 us)
Async XLA Ops:
  7.2 30.3 %copy-start = (bf16[128,256]{1,0:T(8,128)(2,1)S(1)}, bf16[128,256]{1,0:T(8,128)(2,1)}, u32[]{:S(2)}) copy-start(bf16[128,256]{1,0:T(8,128)(2,1)} %param.6) | copy-start | bytes 196612
  7.2 87.8 %all-gather.2.cloned.1.call-start = ((), (), s32[]{:S(2)}) async-start(), calls=%async_computation.10 | async-start | bytes 5242880 | tf_op jit(solution)/shard_map/all_gather | solution.py:60
  10.0 3.1 copy-start.1
  13.1 2.0 copy-start.5
  18.0 24.1 %copy-start.4 = (f32[1,8192]{1,0:T(1,128)S(1)}, f32[1,8192]{1,0:T(1,128)}, u32[]{:S(2)}) copy-start(f32[1,8192]{1,0:T(1,128)} %param.11) | copy-start | bytes 98308
  38.3 8.6 %all-to-all-start = ((bf16[4,2,1024]{2,1,0:T(2,128)(2,1)}), bf16[4,2,1024]{2,1,0:T(2,128)(2,1)S(1)}, u32[]{:S(2)}, u32[]{:S(2)}) async-start(bf16[4,2,1024]{2,1,0:T(2,128)(2,1)} %reshape.174), calls=%async_computation | async-start | bytes 32768 | tf_op jit(solution)/shard_map/all_to_all | solution.py:17
  47.5 42.9 %all-to-all-start.2 = ((f32[4,1,2048]{2,1,0:T(1,128)}), f32[4,1,2048]{2,1,0:T(1,128)S(1)}, u32[]{:S(2)}, u32[]{:S(2)}) async-start(f32[4,1,2048]{2,1,0:T(1,128)} %stack.15), calls=%async_computation.2 | async-start | bytes 65536 | tf_op jit(solution)/shard_map/all_to_all | solution.py:66
  104.0 11.1 %all-to-all-start.3 = ((f32[4,72,128]{2,1,0:T(8,128)}), f32[4,72,128]{2,1,0:T(8,128)S(1)}, u32[]{:S(2)}, u32[]{:S(2)}) async-start(f32[4,72,128]{2,1,0:T(8,128)} %pad_maximum_fusion), calls=%async_computation.3 | async-start | bytes 294912 | tf_op jit(solution)/shard_map/all_to_all | solution.py:17
  150.4 10.9 %all-to-all-start.4 = ((f32[4,72,128]{2,1,0:T(8,128)}), f32[4,72,128]{2,1,0:T(8,128)S(1)}, u32[]{:S(2)}, u32[]{:S(2)}) async-start(f32[4,72,128]{2,1,0:T(8,128)} %pad_maximum_fusion.1), calls=%async_computation.4 | async-start | bytes 294912 | tf_op jit(solution)/shard_map/all_to_all | solution.py:17
  193.6 9.5 %all-to-all-start.5 = ((f32[4,72,128]{2,1,0:T(8,128)}), f32[4,72,128]{2,1,0:T(8,128)S(1)}, u32[]{:S(2)}, u32[]{:S(2)}) async-start(f32[4,72,128]{2,1,0:T(8,128)} %pad_maximum_fusion.2), calls=%async_computation.5 | async-start | bytes 294912 | tf_op jit(solution)/shard_map/all_to_all | solution.py:17
  236.0 9.5 %all-to-all-start.6 = ((f32[4,72,128]{2,1,0:T(8,128)}), f32[4,72,128]{2,1,0:T(8,128)S(1)}, u32[]{:S(2)}, u32[]{:S(2)}) async-start(f32[4,72,128]{2,1,0:T(8,128)} %pad_maximum_fusion.3), calls=%async_computation.6 | async-start | bytes 294912 | tf_op jit(solution)/shard_map/all_to_all | solution.py:17
  252.8 5.8 %copy-start.3 = (bf16[1,128,256]{2,1,0:T(8,128)(2,1)S(1)}, bf16[1,128,256]{2,1,0:T(8,128)(2,1)}, u32[]{:S(2)}) copy-start(bf16[1,128,256]{2,1,0:T(8,128)(2,1)} %param.7) | copy-start | bytes 196612
  252.8 46.4 %all-to-all-start.7 = ((bf16[16,576,128]{2,1,0:T(8,128)(2,1)}), bf16[16,576,128]{2,1,0:T(8,128)(2,1)}, u32[]{:S(2)}, u32[]{:S(2)}) async-start(bf16[16,576,128]{2,1,0:T(8,128)(2,1)} %maximum_maximum_fusion), calls=%async_computation.7 | async-start | bytes 4718592 | tf_op jit(solution)/shard_map/all_to_all | solution.py:17
  301.0 2.0 copy-start.2
  311.4 24.5 %all-to-all-start.8 = ((f32[32,8,128]{2,1,0:T(8,128)}), f32[32,8,128]{2,1,0:T(8,128)S(1)}, u32[]{:S(2)}, u32[]{:S(2)}) async-start(f32[32,8,128]{2,1,0:T(8,128)} %broadcast_in_dim_broadcast_in_dim_broadcast_in_dim.2), calls=%async_computation.8 | async-start | bytes 262144 | tf_op jit(solution)/shard_map/all_to_all | solution.py:17
  336.6 8.6 %all-to-all-start.9 = ((f32[4,8,128]{2,1,0:T(8,128)}), f32[4,8,128]{2,1,0:T(8,128)S(1)}, u32[]{:S(2)}, u32[]{:S(2)}) async-start(f32[4,8,128]{2,1,0:T(8,128)} %broadcast_in_dim.30), calls=%async_computation.9 | async-start | bytes 32768 | tf_op jit(solution)/shard_map/all_to_all | solution.py:17
Sparse Core Ops, SparseCore 0:
  37.6 57.3 all-gather.1
